TPU v7x, 512 devices: a whole 4x4x16 slice. The times are simulated.
512 devices in a mesh: group: 32 (over x, y, core), tp: 16 (over z).
Axes of the slice: x: 4, y: 4, z: 16, core: 2. Of those that a mesh axis runs over, the one named last changes fastest.
Arguments:
- tokens: bfloat16 [24576, 8192], P('group', 'tp'), may hold values from -6 to 6
- w_query: bfloat16 [8192, 4096], P(None, 'tp'), may hold values from -0.0625 to 0.0625
- adapter_down: bfloat16 [384, 16, 8192], P('group', None, 'tp'), may hold values from -0.0625 to 0.0625
- adapter_up: bfloat16 [384, 16, 4096], P('group', None, 'tp'), may hold values from -1.5 to 1.5
- adapter_id: int32 [24576], P('group'), may hold values from 0 to 383, as said below
Outputs:
- query: bfloat16 [24576, 4096], P('group', 'tp')
Inputs may be any that keep to these rules, and one draw needn't show every extreme that they name: `adapter_id`: adapter a is owned by group a // 12. Among the 768 requests of one group (an aligned block), at most 48 use adapters of any one owner; in every draw one owner receives exactly 48 from every group.
All inputs are finite; a program needn't handle non-finite values.
Results may differ from a plain program's by a relative error of at most 0.014.
Values may be sent and summed in bfloat16 or wider, within the bound.
No kernel may reach another device: no remote copies, remote signals or barrier semaphores. Data moves between devices by JAX's collectives and lax.ppermute only.
A program may use at most 128 MiB of HBM per device.

v0:
```python
import jax
import jax.numpy as jnp
from jax import lax
from jax.sharding import PartitionSpec as P

adapter_scale_factor = 2.0
owner_slots = 48
F32, BF16 = (jnp.float32, jnp.bfloat16)


def slot_of_request(adapter_id, groups, per_group):
    n = adapter_id.shape[0]
    owner = adapter_id // per_group
    to_owner = owner[:, None] == lax.broadcasted_iota(jnp.int32, (n, groups), 1)
    before = lax.broadcasted_iota(jnp.int32, (n, n), 0) > lax.broadcasted_iota(jnp.int32, (n, n), 1)
    count = jnp.dot(before.astype(BF16), to_owner.astype(BF16), preferred_element_type=F32)
    rank = jnp.sum(jnp.where(to_owner, count, 0.0), axis=1).astype(jnp.int32)
    return owner * owner_slots + rank


def lora(tokens, adapter_down, adapter_up, adapter_id, groups, tp):
    n, d = tokens.shape
    per_group, rank, _ = adapter_down.shape
    ho = adapter_up.shape[2]
    slots = groups * owner_slots
    slot = slot_of_request(adapter_id, groups, per_group)
    place = (lax.broadcasted_iota(jnp.int32, (slots, n), 0) == slot[None, :]).astype(BF16)
    out_rows = jnp.dot(place, tokens, preferred_element_type=F32).astype(BF16)
    local = (adapter_id % per_group).astype(BF16)
    out_ids = jnp.dot(place, local[:, None], preferred_element_type=F32).astype(BF16)
    out_ids = out_ids.reshape(groups, 1, owner_slots)
    out_ids = jnp.pad(out_ids, ((0, 0), (0, 7), (0, d - owner_slots)))
    sent = jnp.concatenate([out_rows.reshape(groups, owner_slots, d), out_ids], axis=1)
    here = lax.all_to_all(sent, "group", 0, 0, tiled=True)
    rows = here[:, :owner_slots].reshape(slots, d)
    ids = here[:, owner_slots, :owner_slots].astype(jnp.int32).reshape(1, 1, slots)
    mine = lax.broadcasted_iota(jnp.int32, (per_group, 1, slots), 0) == ids
    part = lax.dot_general(
        adapter_down.reshape(per_group * rank, d),
        rows,
        (((1,), (1,)), ((), ())),
        preferred_element_type=F32,
    ).reshape(per_group, rank, slots)
    part = jnp.sum(jnp.where(mine, part, 0.0), axis=0)
    share = rank // tp
    part = lax.all_to_all(part.astype(BF16).reshape(tp, share, slots), "tp", 0, 0, tiled=True)
    scaled = (adapter_scale_factor * jnp.sum(part.astype(F32), axis=0)).astype(BF16)
    scaled = lax.all_to_all(
        jnp.broadcast_to(scaled[None], (tp, share, slots)), "tp", 0, 0, tiled=True
    ).reshape(1, rank, slots)
    spread = jnp.where(mine, scaled, jnp.zeros((), BF16)).reshape(per_group * rank, slots)
    delta = lax.dot_general(
        spread,
        adapter_up.reshape(per_group * rank, ho),
        (((0,), (0,)), ((), ())),
        preferred_element_type=F32,
    ).astype(BF16)
    delta = lax.all_to_all(delta.reshape(groups, owner_slots, ho), "group", 0, 0, tiled=True)
    return lax.dot_general(
        place, delta.reshape(slots, ho), (((0,), (0,)), ((), ())), preferred_element_type=F32
    ).astype(BF16)


def solution(mesh):
    groups, tp = (mesh.shape["group"], mesh.shape["tp"])

    def on_device(tokens, w_query, adapter_down, adapter_up, adapter_id):
        gathered = lax.all_gather(tokens, "tp", axis=1, tiled=True)
        delta = lora(tokens, adapter_down, adapter_up, adapter_id, groups, tp)
        delta, gathered = lax.optimization_barrier((delta, gathered))
        base = lax.optimization_barrier(jnp.dot(gathered, w_query, preferred_element_type=F32))
        return (base + delta.astype(F32)).astype(BF16)

    placed = (
        P("group", "tp"),
        P(None, "tp"),
        P("group", None, "tp"),
        P("group", None, "tp"),
        P("group"),
    )
    return jax.shard_map(
        on_device, mesh=mesh, in_specs=placed, out_specs=P("group", "tp"), check_vma=False
    )
```

profile of v0, /device:TPU:1, one launch (start us, length us, event | category | flops | bytes accessed | tf_op | source)
XLA Modules:
  0.0 182.4 jit_solution(1290667721489595639)
XLA Ops:
  6.5 0.0 copy-start
  6.5 0.0 copy-start.1
  6.5 0.0 all-gather.2.cloned.1.call-start
  6.5 0.7 all-gather.2.cloned.1.call-update
  7.3 0.7 add_select_fusion.1
  8.0 0.4 fusion.13
  8.3 0.7 convert_add_fusion
  9.0 0.9 fusion.14
  9.9 0.1 reshape.91
  10.0 0.0 copy-done.1
  10.0 1.4 fusion.4
  11.4 0.1 fusion.10
  11.6 35.1 %all_to_all.20 = bf16[32,56,512]{2,1,0:T(8,128)(2,1)S(1)} all-to-all(bf16[32,56,512]{2,1,0:T(8,128)(2,1)S(1)} %fusion.10), channel_id=1, replica_groups=mesh['group'=32,'tp'=16] {'group'}, dimensions={0} | all-to-all | bytes 3670016 | tf_op jit(solution)/shard_map/all_to_all | solution.py:34
  46.7 0.1 fusion.20
  46.8 0.1 reshape.86
  46.8 0.2 slice.9
  47.0 0.0 copy-done
  47.0 0.7 fusion.24
  47.7 0.0 copy-start.2
  47.7 0.1 select_reduce_fusion
  47.9 0.5 broadcast.31
  48.4 0.7 reduce.7
  49.1 25.2 %all_to_all.21 = bf16[16,2,768]{2,1,0:T(2,128)(2,1)S(1)} all-to-all(bf16[16,2,768]{2,1,0:T(2,128)(2,1)S(1)} %reshape.99), channel_id=1, replica_groups=mesh['group'=32,'tp'=16] {'tp'}, dimensions={0} | all-to-all | bytes 98304 | tf_op jit(solution)/shard_map/all_to_all | solution.py:46
  74.3 0.1 convert_reduce_fusion
  74.5 0.1 broadcast_in_dim.48
  74.5 0.9 reduce.8
  75.5 15.6 %all_to_all.22 = bf16[16,2,768]{2,1,0:T(2,128)(2,1)S(1)} all-to-all(bf16[16,2,768]{2,1,0:T(2,128)(2,1)S(1)} %reshape.101), channel_id=1, replica_groups=mesh['group'=32,'tp'=16] {'tp'}, dimensions={0} | all-to-all | bytes 98304 | tf_op jit(solution)/shard_map/all_to_all | solution.py:48
  91.1 0.0 copy-done.2
  91.2 0.4 fusion.5
  91.6 19.7 %all_to_all.23 = bf16[32,48,256]{2,1,0:T(8,128)(2,1)S(1)} all-to-all(bf16[32,48,256]{2,1,0:T(8,128)(2,1)S(1)} %bitcast.30), channel_id=1, replica_groups=mesh['group'=32,'tp'=16] {'group'}, dimensions={0} | all-to-all | bytes 1572864 | tf_op jit(solution)/shard_map/all_to_all | solution.py:58
  111.3 1.4 fusion.11
  112.7 54.4 %all-gather.2.cloned.1.call-done = bf16[768,8192]{1,0:T(8,128)(2,1)} async-done(((bf16[768,512]{1,0:T(8,128)(2,1)}), bf16[768,8192]{1,0:T(8,128)(2,1)}) %all-gather.2.cloned.1.call-update) | async-done | bytes 12582928 | tf_op jit(solution)/shard_map/all_gather | solution.py:68
  167.0 7.6 %fusion.25 = f32[768,256]{1,0:T(8,128)S(1)} fusion(bf16[768,8192]{1,0:T(8,128)(2,1)} %all-gather.2.cloned.1.call-done, bf16[8192,256]{1,0:T(8,128)(2,1)} %param.6), kind=kOutput, calls=%fused_computation.43 | convolution fusion | flops 3221225472 | bytes 17563648 | tf_op jit(solution)/shard_map/dot_general | solution.py:71
  174.7 0.9 add_convert_fusion
  (8 shorter events, 0.2 us)
Async XLA Ops:
  6.5 40.5 %copy-start = (bf16[12,16,512]{2,1,0:T(8,128)(2,1)S(1)}, bf16[12,16,512]{2,1,0:T(8,128)(2,1)}, u32[]{:S(2)}) copy-start(bf16[12,16,512]{2,1,0:T(8,128)(2,1)} %param.7) | copy-start | bytes 589828
  6.5 3.5 %copy-start.1 = (bf16[768,512]{1,0:T(8,128)(2,1)S(1)}, bf16[768,512]{1,0:T(8,128)(2,1)}, u32[]{:S(2)}) copy-start(bf16[768,512]{1,0:T(8,128)(2,1)} %param.5) | copy-start | bytes 2359300
  6.5 160.5 %all-gather.2.cloned.1.call-start = ((), (), s32[]{:S(2)}) async-start(), calls=%async_computation.4 | async-start | bytes 13369344 | tf_op jit(solution)/shard_map/all_gather | solution.py:68
  47.7 43.5 %copy-start.2 = (bf16[12,16,256]{2,1,0:T(8,128)(2,1)S(1)}, bf16[12,16,256]{2,1,0:T(8,128)(2,1)}, u32[]{:S(2)}) copy-start(bf16[12,16,256]{2,1,0:T(8,128)(2,1)} %param.8) | copy-start | bytes 294916
Sparse Core Ops, SparseCore 0:
  9.4 157.5 all-gather.1
where the time goes:
time: 183 us; the launch traced here: 182 us
  blocking collectives  95.6 us (52%)
  waiting for transfers between devices  55.1 us (30%)
  between operations  13.6 us (7%)
  matrix products  12.8 us (7%)
  other arithmetic  4.3 us (2%)
    all_gather x1, waiting for transfers between devices, on_device(): gathered = lax.all_gather(tokens, 'tp', axis=1, tiled=True)  54.4 us
    all_to_all x1, blocking collectives, lora(): here = lax.all_to_all(sent, 'group', 0, 0, tiled=True)  35.1 us
    all_to_all x1, blocking collectives, lora(): lax.all_to_all(part.astype(BF16).reshape(tp, share, slots), 'tp', 0, 0, t...  25.2 us
    all_to_all x1, blocking collectives, lora(): lax.all_to_all(delta.reshape(groups, owner_slots, ho), 'group', 0, 0, til...  19.7 us
    all_to_all x1, blocking collectives, lora(): lax.all_to_all(jnp.broadcast_to(scaled[None], (tp, share, slots)), 'tp',...  15.6 us
    dot_general x1, matrix products, on_device(): jnp.dot(gathered, w_query, preferred_element_type=F32)  7.62 us
  transfers between devices with their start and end apart: 1, of which 1 were waited for; matrix products, arithmetic and copies ran while one was open for 5% of the time, Pallas kernels for 0%

commit v1 on v0

--- a/solution.py
+++ b/solution.py
@@ -6,6 +6,12 @@
 adapter_scale_factor = 2.0
 owner_slots = 48
 F32, BF16 = (jnp.float32, jnp.bfloat16)
+
+
+def gather_from_all(x, axis, dim):
+    size = lax.axis_size(axis)
+    repeats = [size if d == dim else 1 for d in range(x.ndim)]
+    return lax.all_to_all(jnp.tile(x, repeats), axis, split_axis=dim, concat_axis=dim, tiled=True)
 
 
 def slot_of_request(adapter_id, groups, per_group):
@@ -65,7 +71,7 @@
     groups, tp = (mesh.shape["group"], mesh.shape["tp"])
 
     def on_device(tokens, w_query, adapter_down, adapter_up, adapter_id):
-        gathered = lax.all_gather(tokens, "tp", axis=1, tiled=True)
+        gathered = gather_from_all(tokens, "tp", 1)
         delta = lora(tokens, adapter_down, adapter_up, adapter_id, groups, tp)
         delta, gathered = lax.optimization_barrier((delta, gathered))
         base = lax.optimization_barrier(jnp.dot(gathered, w_query, preferred_element_type=F32))

time: 183 us -> 682 us (3.73)
  waiting for transfers between devices: 55.1 us -> 541 us
  local copies, waits for them, and re-layouts: 1.05 us -> 23.4 us
  between operations: 13.6 us -> 0.18 us
    all_to_all x0 -> x1, waiting for transfers between devices: none -> 541 us  [gather_from_all(): lax.all_to_all(jnp.tile(x, repeats), axis, split_axis=dim, concat_axis=di...]
    all_gather x1 -> x0, waiting for transfers between devices: 54.4 us -> none  [on_device(): gathered = lax.all_gather(tokens, 'tp', axis=1, tiled=True)]
    all_to_all x0 -> x1, local copies, waits for them, and re-layouts: none -> 16.6 us  [gather_from_all(): lax.all_to_all(jnp.tile(x, repeats), axis, split_axis=dim, concat_axis=di...]
  transfers between devices with their start and end apart: 1 -> 1, of which waited for: 1 -> 1; matrix products, arithmetic and copies ran while one was open for 5% -> 0% of each run, Pallas kernels for 0% -> 0%
where the time goes in v1:
time: 682 us; the launch traced here: 681 us
  waiting for transfers between devices  541 us (79%)
  blocking collectives  94.6 us (14%)
  local copies, waits for them, and re-layouts  23.4 us (3%)
  matrix products  12.8 us (2%)
    all_to_all x1, waiting for transfers between devices, gather_from_all(): lax.all_to_all(jnp.tile(x, repeats), axis, split_axis=dim, concat_axis=di...  541 us
    all_to_all x1, blocking collectives, lora(): here = lax.all_to_all(sent, 'group', 0, 0, tiled=True)  35.1 us
    all_to_all x1, blocking collectives, lora(): lax.all_to_all(part.astype(BF16).reshape(tp, share, slots), 'tp', 0, 0, t...  25.1 us
    all_to_all x1, blocking collectives, lora(): lax.all_to_all(delta.reshape(groups, owner_slots, ho), 'group', 0, 0, til...  19.7 us
    all_to_all x1, local copies, waits for them, and re-layouts, gather_from_all(): lax.all_to_all(jnp.tile(x, repeats), axis, split_axis=dim, concat_axis=di...  16.6 us
    all_to_all x1, blocking collectives, lora(): lax.all_to_all(jnp.broadcast_to(scaled[None], (tp, share, slots)), 'tp',...  14.7 us
  transfers between devices with their start and end apart: 1, of which 1 were waited for; matrix products, arithmetic and copies ran while one was open for 0% of the time, Pallas kernels for 0%

profile of v1, /device:TPU:1, one launch (start us, length us, event | category | flops | bytes accessed | tf_op | source)
XLA Modules:
  0.0 681.3 jit_solution(5645672909503928412)
XLA Ops:
  0.0 0.0 copy-start
  0.0 0.0 copy-start.1
  0.0 0.8 add_select_fusion.1
  0.8 0.4 fusion.13
  1.1 0.7 convert_add_fusion
  1.9 0.9 fusion.14
  2.8 0.1 reshape.98
  2.9 0.0 copy-done.1
  2.9 1.4 fusion.4
  4.3 0.1 fusion.10
  4.4 35.1 %all_to_all.29 = bf16[32,56,512]{2,1,0:T(8,128)(2,1)S(1)} all-to-all(bf16[32,56,512]{2,1,0:T(8,128)(2,1)S(1)} %fusion.10), channel_id=1, replica_groups=mesh['group'=32,'tp'=16] {'group'}, dimensions={0} | all-to-all | bytes 3670016 | tf_op jit(solution)/shard_map/all_to_all | solution.py:40
  39.5 0.1 fusion.20
  39.6 0.1 reshape.93
  39.7 0.2 slice.9
  39.9 0.0 copy-done
  39.9 0.7 fusion.24
  40.5 0.0 copy-start.2
  40.6 0.1 select_reduce_fusion
  40.7 0.5 broadcast.34
  41.2 0.7 reduce.7
  41.9 25.1 %all_to_all.30 = bf16[16,2,768]{2,1,0:T(2,128)(2,1)S(1)} all-to-all(bf16[16,2,768]{2,1,0:T(2,128)(2,1)S(1)} %reshape.106), channel_id=1, replica_groups=mesh['group'=32,'tp'=16] {'tp'}, dimensions={0} | all-to-all | bytes 98304 | tf_op jit(solution)/shard_map/all_to_all | solution.py:52
  67.0 0.1 convert_reduce_fusion
  67.1 0.1 broadcast_in_dim.48
  67.2 0.9 reduce.8
  68.1 14.7 %all_to_all.31 = bf16[16,2,768]{2,1,0:T(2,128)(2,1)S(1)} all-to-all(bf16[16,2,768]{2,1,0:T(2,128)(2,1)S(1)} %reshape.108), channel_id=1, replica_groups=mesh['group'=32,'tp'=16] {'tp'}, dimensions={0} | all-to-all | bytes 98304 | tf_op jit(solution)/shard_map/all_to_all | solution.py:54
  82.9 0.0 copy-done.2
  82.9 0.4 fusion.5
  83.3 19.7 %all_to_all.32 = bf16[32,48,256]{2,1,0:T(8,128)(2,1)S(1)} all-to-all(bf16[32,48,256]{2,1,0:T(8,128)(2,1)S(1)} %bitcast.33), channel_id=1, replica_groups=mesh['group'=32,'tp'=16] {'group'}, dimensions={0} | all-to-all | bytes 1572864 | tf_op jit(solution)/shard_map/all_to_all | solution.py:64
  103.0 5.7 tile.2
  108.7 4.9 all-to-all-start.4
  113.7 1.4 fusion.11
  115.1 541.0 %all-to-all-done.4 = bf16[768,16,512]{2,0,1:T(8,128)(2,1)} async-done(((bf16[768,16,512]{2,0,1:T(8,128)(2,1)}), bf16[768,16,512]{2,0,1:T(8,128)(2,1)}, u32[]{:S(2)}, u32[]{:S(2)}) %all-to-all-start.4) | async-done | bytes 12582944 | tf_op jit(solution)/shard_map/all_to_all | solution.py:14
  656.1 16.6 %copy.10 = bf16[768,16,512]{0,2,1:T(8,128)(2,1)} copy(bf16[768,16,512]{2,0,1:T(8,128)(2,1)} %all-to-all-done.4) | data formatting | bytes 25165824 | tf_op jit(solution)/shard_map/all_to_all | solution.py:14
  672.7 7.7 %fusion.25 = f32[768,256]{1,0:T(8,128)S(1)} fusion(bf16[768,8192]{0,1:T(8,128)(2,1)} %bitcast.28, bf16[8192,256]{1,0:T(8,128)(2,1)} %param.6), kind=kOutput, calls=%fused_computation.43 | convolution fusion | flops 3221225472 | bytes 17563648 | tf_op jit(solution)/shard_map/dot_general | solution.py:77
  680.4 0.9 add_convert_fusion
  (8 shorter events, 0.2 us)
Async XLA Ops:
  0.0 39.9 %copy-start = (bf16[12,16,512]{2,1,0:T(8,128)(2,1)S(1)}, bf16[12,16,512]{2,1,0:T(8,128)(2,1)}, u32[]{:S(2)}) copy-start(bf16[12,16,512]{2,1,0:T(8,128)(2,1)} %param.7) | copy-start | bytes 589828
  0.0 2.9 copy-start.1
  40.5 42.4 %copy-start.2 = (bf16[12,16,256]{2,1,0:T(8,128)(2,1)S(1)}, bf16[12,16,256]{2,1,0:T(8,128)(2,1)}, u32[]{:S(2)}) copy-start(bf16[12,16,256]{2,1,0:T(8,128)(2,1)} %param.8) | copy-start | bytes 294916
  108.7 547.4 %all-to-all-start.4 = ((bf16[768,16,512]{2,0,1:T(8,128)(2,1)}), bf16[768,16,512]{2,0,1:T(8,128)(2,1)}, u32[]{:S(2)}, u32[]{:S(2)}) async-start(bf16[768,16,512]{2,0,1:T(8,128)(2,1)} %tile.2), calls=%async_computation.4 | async-start | bytes 25165824 | tf_op jit(solution)/shard_map/all_to_all | solution.py:14
